TPU v7x, 32 devices: a whole 2x2x4 slice. The times are simulated.
32 devices in a mesh: gx: 8 (over y, x, core), gy: 4 (over z).
Axes of the slice: x: 2, y: 2, z: 4, core: 2. Of those that a mesh axis runs over, the one named last changes fastest.
Arguments:
- source: float32 [160, 80, 640], P('gx', 'gy'), may hold values from -210 to 210
- conductivity: float32 [160, 80, 640], P('gx', 'gy'), may hold values from 0.001 to 1
- absorption: float32 [160, 80, 640], P('gx', 'gy'), may hold values from 1 to 10
Outputs:
- solution: float32 [160, 80, 640], P('gx', 'gy')
- correction: float32 [96, 48, 384], P('gx', 'gy')
All inputs are finite; a program needn't handle non-finite values.
Results may differ from a plain program's by a relative error of at most 0.00023.
Values sent between devices are 32-bit elements; how exact they have to be, the bound alone decides.
A program may use at most 128 MiB of HBM per device.

v0:
```python
import functools
import math

import jax
import jax.numpy as jnp
import numpy as np
from jax import lax
from jax.experimental import pallas as pl
from jax.experimental.pallas import tpu as pltpu
from jax.sharding import PartitionSpec as P

SWEEPS = 3
STAGES = 7
MESH = pl.DeviceIdType.MESH
DIRS = [(-1, 0), (1, 0), (0, -1), (0, 1), (-1, -1), (-1, 1), (1, -1), (1, 1)]


def deriv_table(points):
    count = len(points)
    barycentric = np.array(
        [
            1.0 / np.prod([points[j] - points[k] for k in range(count) if k != j])
            for j in range(count)
        ]
    )
    table = np.zeros((count, count))
    for i in range(count):
        for j in range(count):
            if i != j:
                table[i, j] = barycentric[j] / (barycentric[i] * (points[i] - points[j]))
        table[i, i] = -np.sum(table[i])
    return table


ROOT = math.sqrt(3.0 / 7.0)
FINE_POINTS = np.array([-1.0, -ROOT, 0.0, ROOT, 1.0])
FINE_W = np.array([0.1, 49.0 / 90.0, 32.0 / 45.0, 49.0 / 90.0, 0.1])
COARSE_POINTS = np.array([-1.0, 0.0, 1.0])
COARSE_W = np.array([1.0 / 3.0, 4.0 / 3.0, 1.0 / 3.0])
FINE_D = deriv_table(FINE_POINTS)
COARSE_D = deriv_table(COARSE_POINTS)
INTERP = np.stack(
    [
        FINE_POINTS * (FINE_POINTS - 1.0) / 2.0,
        1.0 - FINE_POINTS**2,
        FINE_POINTS * (FINE_POINTS + 1.0) / 2.0,
    ],
    1,
)
RESTRICT = INTERP.T * np.array([0.5, 1.0, 1.0, 1.0, 0.5])[None, :]
QF, QC = 5, 3


def chebyshev_coefficients():
    theta, delta, sigma, rho = 0.75, 0.45, 5.0 / 3.0, 0.6
    x = np.zeros(SWEEPS + 1)
    r = np.zeros(SWEEPS + 1)
    r[0] = 1.0
    d = r / theta
    for sweep in range(SWEEPS):
        x = x + d
        r = r - np.concatenate([[0.0], d[:-1]])
        if sweep + 1 < SWEEPS:
            rho_next = 1.0 / (2.0 * sigma - rho)
            d = rho_next * rho * d + 2.0 * rho_next / delta * r
            rho = rho_next
    return [float(v) for v in x[:SWEEPS]]


CHEB = chebyshev_coefficients()


def antisym(table, u):
    n = len(u)
    half = n // 2
    even = [u[j] + u[n - 1 - j] for j in range(half)]
    odd = [u[j] - u[n - 1 - j] for j in range(half)]
    out = [None] * n
    for i in range(half):
        p = float(table[i, half]) * u[half]
        q = None
        for j in range(half):
            s = (table[i, j] + table[i, n - 1 - j]) / 2
            t = (table[i, j] - table[i, n - 1 - j]) / 2
            p = p + float(s) * even[j]
            q = float(t) * odd[j] if q is None else q + float(t) * odd[j]
        out[i] = q + p
        out[n - 1 - i] = q - p
    mid = None
    for j in range(half):
        term = float(table[half, j]) * odd[j]
        mid = term if mid is None else mid + term
    out[half] = mid
    return out


def dense(table, u):
    out = []
    for i in range(table.shape[0]):
        acc = None
        for j in range(table.shape[1]):
            c = float(table[i, j])
            if abs(c) < 1e-14:
                continue
            term = u[j] if c == 1.0 else c * u[j]
            acc = term if acc is None else acc + term
        out.append(acc)
    return out


def plane_starts(q, axis, a, b):
    strides = (q * q, q, 1)
    other = [s for k, s in enumerate(strides) if k != axis]
    return a * other[0] + b * other[1], strides[axis]


def z_sum(line, lanes):
    lo, hi = line[0], line[-1]
    line[-1] = hi + pltpu.roll(lo, lanes - 1, 1)
    line[0] = lo + pltpu.roll(hi, 1, 1)
    return line


def local_op(src, dst, flux, mass, table, lanes):
    q = table.shape[0]
    for axis in range(3):

        @pl.loop(0, q)
        def _(a, axis=axis):
            for b in range(q):
                start, step = plane_starts(q, axis, a, b)
                u = [src[start + step * i] for i in range(q)]
                g = antisym(table, u)
                g = [flux[start + step * i] * g[i] for i in range(q)]
                r = antisym(table.T, g)
                for i in range(q):
                    base = mass[start + step * i] * u[i] if axis == 0 else dst[start + step * i]
                    r[i] = base + r[i]
                if axis == 2:
                    r = z_sum(r, lanes)
                for i in range(q):
                    dst[start + step * i] = r[i]


def local_diag(dst, flux, mass, table, lanes):
    q = table.shape[0]
    square = (table * table).T
    for axis in range(3):

        @pl.loop(0, q)
        def _(a, axis=axis):
            for b in range(q):
                start, step = plane_starts(q, axis, a, b)
                r = dense(square, [flux[start + step * i] for i in range(q)])
                for i in range(q):
                    base = mass if axis == 0 else dst
                    r[i] = base[start + step * i] + r[i]
                if axis == 2:
                    r = z_sum(r, lanes)
                for i in range(q):
                    dst[start + step * i] = r[i]


def kernel(
    nx,
    ny,
    src_ref,
    cond_ref,
    abs_ref,
    out_ref,
    cor_ref,
    wide,
    raw,
    craw,
    perm,
    back,
    cback,
    fine,
    flux,
    mass,
    coarse,
    cflux,
    cmass,
    tmp_a,
    tmp_b,
    send,
    recv,
    line_x_send,
    line_x,
    line_y_send,
    line_y,
    send_sem,
    recv_sem,
    line_send_sem,
    line_x_sem,
    line_y_sem,
):
    px, py, pz = src_ref.shape
    ex, ey, ez = px // QF, py // QF, pz // QF
    subs, lanes = ex * ey, ez
    rows_x = -(-py // 8) * 8
    rows = px * rows_x
    mx, my = lax.axis_index("gx"), lax.axis_index("gy")

    def target(dx, dy):
        return (lax.rem(mx + dx + nx, nx), lax.rem(my + dy + ny, ny))

    greeted = {(o, 0) for o in range(1, nx)} | {(0, o) for o in range(1, ny)}
    greeted |= {(dx % nx, dy % ny) for dx, dy in DIRS}
    greeted = sorted(greeted)
    barrier = pltpu.get_barrier_semaphore()
    for dx, dy in greeted:
        pl.semaphore_signal(barrier, inc=1, device_id=target(dx, dy), device_id_type=MESH)

    sub = lax.broadcasted_iota(jnp.int32, (subs, lanes), 0)

    def any_of(indices):
        mask = None
        for index in indices:
            one = sub == index
            mask = one if mask is None else mask | one
        return mask

    x_group = [(sub >= j * ey) & (sub < (j + 1) * ey) for j in range(ex)]
    y_group = [any_of([e * ey + j for e in range(ex)]) for j in range(ey)]
    at_sub = {}

    def single(index):
        if index not in at_sub:
            at_sub[index] = sub == index
        return at_sub[index]

    def shifted(plane, shift):
        shift = shift % subs
        return plane if shift == 0 else pltpu.roll(plane, shift, 0)

    def layout(d):
        dx, dy = DIRS[d]
        if dy == 0:
            return ex, ey, (0 if dx < 0 else ex - 1), (ex - 1 if dx < 0 else 0)
        if dx == 0:
            return ey, 1, (0 if dy < 0 else ey - 1), (ey - 1 if dy < 0 else 0)
        sx, tx = (0, ex - 1) if dx < 0 else (ex - 1, 0)
        sy, ty = (0, ey - 1) if dy < 0 else (ey - 1, 0)
        return subs, 1, sx * ey + sy, tx * ey + ty

    def group_mask(d, j):
        dx, dy = DIRS[d]
        if dy == 0:
            return x_group[j]
        if dx == 0:
            return y_group[j]
        return single(j)

    def face_planes(d, q):
        dx, dy = DIRS[d]
        xs = range(q) if dx == 0 else [0 if dx < 0 else q - 1]
        ys = range(q) if dy == 0 else [0 if dy < 0 else q - 1]
        return [(x * q + y) * q + z for x in xs for y in ys for z in range(q)]

    def copy_of(stage, d, tiles):
        return pltpu.make_async_remote_copy(
            src_ref=send.at[stage, d, pl.ds(0, tiles)],
            dst_ref=recv.at[stage, d, pl.ds(0, tiles)],
            send_sem=send_sem.at[stage, d],
            recv_sem=recv_sem.at[stage, d],
            device_id=target(*DIRS[d]),
            device_id_type=MESH,
        )

    pending = []

    def start_exchange(stage, fields):
        copies = []
        for d in range(len(DIRS)):
            groups, distance, source, _ = layout(d)
            planes = [ref.at[p] for ref, q in fields for p in face_planes(d, q)]
            tiles = -(-len(planes) // groups)
            for t in range(tiles):
                acc = None
                for j, plane in enumerate(planes[t * groups : (t + 1) * groups]):
                    moved = shifted(plane[...], (j - source) * distance)
                    acc = moved if acc is None else jnp.where(group_mask(d, j), moved, acc)
                send[stage, d, t] = acc
            copy = copy_of(stage, d, tiles)
            copy.start()
            copies.append(copy)
        return copies

    not_first_x, not_last_x = sub >= ey, sub < (ex - 1) * ey
    first_y, last_y = y_group[0], y_group[ey - 1]

    def finish_exchange(stage, fields, copies):
        for copy in copies:
            copy.wait_recv()
        pending.extend(copies)

        def received(d, number):
            groups, distance, _, place = layout(d)
            tile, j = divmod(number, groups)
            return shifted(recv[stage, d, tile], (place - j) * distance)

        offsets = [0] * len(DIRS)
        for ref, q in fields:
            last = q - 1
            plane = lambda x, y, z: (x * q + y) * q + z

            def x_sum(lo, hi, from_low, from_high):
                new_lo = lo + jnp.where(not_first_x, shifted(hi, ey), from_low)
                new_hi = hi + jnp.where(not_last_x, shifted(lo, -ey), from_high)
                return new_lo, new_hi

            for y in range(q):
                for z in range(q):
                    number = y * q + z
                    lo, hi = x_sum(
                        ref[plane(0, y, z)],
                        ref[plane(last, y, z)],
                        received(1, offsets[1] + number),
                        received(0, offsets[0] + number),
                    )
                    ref[plane(0, y, z)] = lo
                    ref[plane(last, y, z)] = hi
            for z in range(q):
                low = [received(3, offsets[3] + x * q + z) for x in range(q)]
                high = [received(2, offsets[2] + x * q + z) for x in range(q)]
                low[0], low[last] = x_sum(
                    low[0], low[last], received(7, offsets[7] + z), received(5, offsets[5] + z)
                )
                high[0], high[last] = x_sum(
                    high[0], high[last], received(6, offsets[6] + z), received(4, offsets[4] + z)
                )
                for x in range(q):
                    lo, hi = ref[plane(x, 0, z)], ref[plane(x, last, z)]
                    ref[plane(x, 0, z)] = lo + jnp.where(first_y, low[x], shifted(hi, 1))
                    ref[plane(x, last, z)] = hi + jnp.where(last_y, high[x], shifted(lo, -1))
            for d in range(len(DIRS)):
                offsets[d] += len(face_planes(d, q))

    def start_line(which, along_x, first, second):
        out, slots, sems = (
            (line_x_send, line_x, line_x_sem) if along_x else (line_y_send, line_y, line_y_sem)
        )
        count = nx if along_x else ny
        out[which, 0:1] = first
        out[which, 1:2] = second
        copies = []
        for o in range(1, count):
            copy = pltpu.make_async_remote_copy(
                src_ref=out.at[which],
                dst_ref=slots.at[which, o],
                send_sem=line_send_sem.at[which, 0 if along_x else 1, o],
                recv_sem=sems.at[which, o],
                device_id=target(o, 0) if along_x else target(0, o),
                device_id_type=MESH,
            )
            copy.start()
            copies.append(copy)
        return copies

    def finish_line(which, along_x, copies):
        out, slots = (line_x_send, line_x) if along_x else (line_y_send, line_y)
        count = nx if along_x else ny
        for copy in copies:
            copy.wait_recv()
        pending.extend(copies)
        total = out[which]
        for o in range(1, count):
            total = total + slots[which, o]
        return total[0:1], total[1:2]

    def inverse_estimate(first, second):
        first = jnp.sum(first, axis=1, keepdims=True)
        second = jnp.sum(second, axis=1, keepdims=True)
        return 1.0 / jnp.sqrt(second / (first + 1e-06))

    def coefficients(inv_est):
        power = inv_est
        out = []
        for c in CHEB:
            out.append(jnp.broadcast_to(c * power, (subs, lanes)))
            power = power * inv_est
        return out

    for k in range(QF):
        row = lax.broadcasted_iota(jnp.int32, (pz, ez), 0)
        col = lax.broadcasted_iota(jnp.int32, (pz, ez), 1)
        perm[:, k * ez : (k + 1) * ez] = jnp.where(row == QF * col + k, 1.0, 0.0).astype(
            jnp.bfloat16
        )

    def transposed_permutation(ref, q):
        for k in range(q):
            row = lax.broadcasted_iota(jnp.int32, (ez, q * ez), 0)
            col = lax.broadcasted_iota(jnp.int32, (ez, q * ez), 1)
            ref[k * ez : (k + 1) * ez, :] = jnp.where(col == q * row + k, 1.0, 0.0).astype(
                jnp.bfloat16
            )

    def split_dot(value, table):
        high = value.astype(jnp.bfloat16)
        rest = value - high.astype(jnp.float32)
        mid = rest.astype(jnp.bfloat16)
        low = (rest - mid.astype(jnp.float32)).astype(jnp.bfloat16)
        dot = functools.partial(jnp.dot, preferred_element_type=jnp.float32)
        return dot(high, table) + (dot(mid, table) + dot(low, table))

    for n, ref in enumerate((src_ref, cond_ref, abs_ref)):
        for x in range(px):
            wide[n * rows + x * rows_x : n * rows + x * rows_x + py, :] = ref[x]
    chunk = rows // 2

    @pl.loop(0, 6)
    def _(c):
        at = pl.multiple_of(c * chunk, 8)
        moved = split_dot(wide[pl.ds(at, chunk), :], perm[...])
        for k in range(QF):
            raw[k, pl.ds(at, chunk), :] = moved[:, k * ez : (k + 1) * ez]

    pick = {0: 0, 2: 1, 4: 2}
    for x in range(QF):
        for y in range(QF):
            for z in range(QF):
                p = (x * QF + y) * QF + z
                weight = float(FINE_W[x] * FINE_W[y] * FINE_W[z])
                on_coarse = x in pick and y in pick and z in pick
                for e in range(ex):
                    at = (e * QF + x) * rows_x + y
                    values = [
                        raw[z, pl.ds(n * rows + at, ey, stride=QF), :] for n in range(3)
                    ]
                    place = slice(e * ey, (e + 1) * ey)
                    fine[0, p, place, :] = weight * values[0]
                    flux[p, place, :] = weight * values[1]
                    mass[p, place, :] = weight * values[2]
                    if on_coarse:
                        i, j, k = pick[x], pick[y], pick[z]
                        cp = (i * QC + j) * QC + k
                        cw = float(COARSE_W[i] * COARSE_W[j] * COARSE_W[k])
                        cflux[cp, place, :] = cw * values[1]
                        cmass[cp, place, :] = cw * values[2]

    load, inv, power, w0, w1, w2, b = [fine.at[i] for i in range(7)]
    power_2 = fine.at[7]
    cinv, cur, crhs, cw0, cb, cpow, cw1, ccor = [coarse.at[i] for i in range(8)]

    def each(q, body):
        @pl.loop(0, q * q)
        def _(a):
            for i in range(q):
                body(a * q + i)

    def squares(q, values):
        def body(a, acc):
            for i in range(q):
                v = values(a * q + i)
                acc = acc + v * v
            return acc

        total = lax.fori_loop(0, q * q, body, jnp.zeros((subs, lanes), jnp.float32))
        return jnp.sum(total, axis=0, keepdims=True)

    def store(dst, values):
        def body(p):
            dst[p] = values(p)

        return body

    def restrict(field, dst):
        for x in range(1):

            @pl.loop(0, QF)
            def _(a):
                for c in range(QF):
                    line = dense(RESTRICT, [field[i * QF * QF + a * QF + c] for i in range(QF)])
                    for i in range(QC):
                        tmp_a[i * QF * QF + a * QF + c] = line[i]

        @pl.loop(0, QC)
        def _(a):
            for c in range(QF):
                line = dense(RESTRICT, [tmp_a[a * QF * QF + i * QF + c] for i in range(QF)])
                for i in range(QC):
                    tmp_b[a * QC * QF + i * QF + c] = line[i]

        @pl.loop(0, QC)
        def _(a):
            for c in range(QC):
                line = dense(RESTRICT, [tmp_b[a * QC * QF + c * QF + i] for i in range(QF)])
                line = z_sum(line, lanes)
                for i in range(QC):
                    dst[a * QC * QC + c * QC + i] = line[i]

    def apply_fine(src, dst):
        local_op(src, dst, flux, mass, FINE_D, lanes)

    def apply_coarse(src, dst):
        local_op(src, dst, cflux, cmass, COARSE_D, lanes)

    @pl.loop(0, QF * QF)
    def _(a):
        line = z_sum([load[a * QF + i] for i in range(QF)], lanes)
        load[a * QF] = line[0]
        load[a * QF + QF - 1] = line[-1]

    local_diag(inv, flux, mass, FINE_D, lanes)
    local_diag(cinv, cflux, cmass, COARSE_D, lanes)
    pl.semaphore_wait(barrier, len(greeted))
    fields = [(load, QF), (inv, QF), (cinv, QC)]
    copies = start_exchange(0, fields)
    transposed_permutation(back, QF)
    transposed_permutation(cback, QC)
    finish_exchange(0, fields, copies)

    def invert(p):
        value = 1.0 / inv[p]
        inv[p] = value
        b[p] = value * load[p]

    each(QF, invert)
    each(QC, store(cinv, lambda p: 1.0 / cinv[p]))

    apply_fine(load, power)
    apply_fine(b, w0)
    restrict(load, crhs)
    fields = [(power, QF), (w0, QF), (crhs, QC)]
    finish_exchange(1, fields, start_exchange(1, fields))
    each(QF, store(power, lambda p: inv[p] * power[p]))
    each(QF, store(b, lambda p: inv[p] * w0[p]))

    apply_fine(power, power_2)
    apply_fine(b, w1)
    apply_coarse(crhs, cpow)
    fields = [(power_2, QF), (w1, QF), (cpow, QC)]
    copies = start_exchange(2, fields)
    sum_first = squares(QF, lambda p: power[p])
    finish_exchange(2, fields, copies)
    sum_second = squares(QF, lambda p: inv[p] * power_2[p])
    line = start_line(0, True, sum_first, sum_second)
    each(QF, store(b, lambda p: inv[p] * w1[p]))
    each(QC, store(cpow, lambda p: cinv[p] * cpow[p]))

    apply_fine(b, w2)
    line = start_line(0, False, *finish_line(0, True, line))
    apply_coarse(cpow, cur)
    fields = [(w2, QF), (cur, QC)]
    copies = start_exchange(3, fields)
    csum_first = squares(QC, lambda p: cpow[p])
    scale = coefficients(inverse_estimate(*finish_line(0, False, line)))
    finish_exchange(3, fields, copies)
    csum_second = squares(QC, lambda p: cinv[p] * cur[p])
    each(
        QF,
        store(
            b, lambda p: load[p] - (scale[0] * w0[p] + scale[1] * w1[p] + scale[2] * w2[p])
        ),
    )

    restrict(b, crhs)
    fields = [(crhs, QC)]
    copies = start_exchange(4, fields)
    line = start_line(1, True, csum_first, csum_second)
    each(
        QF,
        store(
            power,
            lambda p: inv[p] * (scale[0] * load[p] + scale[1] * w0[p] + scale[2] * w1[p]),
        ),
    )
    finish_exchange(4, fields, copies)
    each(QC, store(cb, lambda p: cinv[p] * crhs[p]))

    apply_coarse(cb, cw0)
    fields = [(cw0, QC)]
    copies = start_exchange(5, fields)
    line = start_line(1, False, *finish_line(1, True, line))
    finish_exchange(5, fields, copies)
    each(QC, store(cb, lambda p: cinv[p] * cw0[p]))

    apply_coarse(cb, cw1)
    fields = [(cw1, QC)]
    copies = start_exchange(6, fields)
    cscale = coefficients(inverse_estimate(*finish_line(1, False, line)))
    finish_exchange(6, fields, copies)
    each(
        QC,
        store(
            ccor,
            lambda p: cinv[p]
            * (cscale[0] * crhs[p] + cscale[1] * cw0[p] + cscale[2] * cw1[p]),
        ),
    )

    for y in range(QC):
        for z in range(QC):
            line = dense(INTERP, [ccor[i * QC * QC + y * QC + z] for i in range(QC)])
            for i in range(QF):
                tmp_a[(i * QC + y) * QC + z] = line[i]
    for x in range(QF):
        for z in range(QC):
            line = dense(INTERP, [tmp_a[(x * QC + i) * QC + z] for i in range(QC)])
            for i in range(QF):
                tmp_b[(x * QF + i) * QC + z] = line[i]
    for x in range(QF):
        for y in range(QF):
            line = dense(INTERP, [tmp_b[(x * QF + y) * QC + i] for i in range(QC)])
            for z in range(QF):
                value = power[(x * QF + y) * QF + z] + line[z]
                for e in range(ex):
                    at = (e * QF + x) * rows_x + y
                    raw[z, pl.ds(at, ey, stride=QF), :] = value[e * ey : (e + 1) * ey]
    crows_x = cor_ref.shape[1] + (-cor_ref.shape[1]) % 8
    for x in range(QC):
        for y in range(QC):
            for z in range(QC):
                value = ccor[(x * QC + y) * QC + z]
                for e in range(ex):
                    at = (e * QC + x) * crows_x + y
                    craw[z, pl.ds(at, ey, stride=QC), :] = value[e * ey : (e + 1) * ey]

    @pl.loop(0, 2)
    def _(c):
        at = pl.multiple_of(c * chunk, 8)
        packed = jnp.concatenate([raw[k, pl.ds(at, chunk), :] for k in range(QF)], axis=1)
        wide[pl.ds(at, chunk), :] = split_dot(packed, back[...])

    for x in range(px):
        out_ref[x] = wide[x * rows_x : x * rows_x + py, :]
    packed = jnp.concatenate([craw[k] for k in range(QC)], axis=1)
    moved = split_dot(packed, cback[...])
    for x in range(cor_ref.shape[0]):
        cor_ref[x] = moved[x * crows_x : x * crows_x + cor_ref.shape[1], :]
    for copy in pending:
        copy.wait_send()


def on_device(nx, ny, source, conductivity, absorption):
    px, py, pz = source.shape
    ex, ey, ez = px // QF, py // QF, pz // QF
    subs = ex * ey
    rows = px * (-(-py // 8) * 8)
    crows = ex * QC * (-(-ey * QC // 8) * 8)
    tiles = -(-(2 * QF * QF + QC * QC) // min(ex, ey))
    f32, bf16 = jnp.float32, jnp.bfloat16
    dirs = len(DIRS)
    longest = max(nx, ny)
    scratch = [
        pltpu.VMEM((3 * rows, pz), f32),
        pltpu.VMEM((QF, 3 * rows, ez), f32),
        pltpu.VMEM((QC, crows, ez), f32),
        pltpu.VMEM((pz, pz), bf16),
        pltpu.VMEM((pz, pz), bf16),
        pltpu.VMEM((QC * ez, QC * ez), bf16),
        pltpu.VMEM((8, QF**3, subs, ez), f32),
        pltpu.VMEM((QF**3, subs, ez), f32),
        pltpu.VMEM((QF**3, subs, ez), f32),
        pltpu.VMEM((8, QC**3, subs, ez), f32),
        pltpu.VMEM((QC**3, subs, ez), f32),
        pltpu.VMEM((QC**3, subs, ez), f32),
        pltpu.VMEM((QF * QF * QC, subs, ez), f32),
        pltpu.VMEM((QF * QF * QC, subs, ez), f32),
        pltpu.VMEM((STAGES, dirs, tiles, subs, ez), f32),
        pltpu.VMEM((STAGES, dirs, tiles, subs, ez), f32),
        pltpu.VMEM((2, 8, ez), f32),
        pltpu.VMEM((2, nx, 8, ez), f32),
        pltpu.VMEM((2, 8, ez), f32),
        pltpu.VMEM((2, ny, 8, ez), f32),
        pltpu.SemaphoreType.DMA((STAGES, dirs)),
        pltpu.SemaphoreType.DMA((STAGES, dirs)),
        pltpu.SemaphoreType.DMA((2, 2, longest)),
        pltpu.SemaphoreType.DMA((2, nx)),
        pltpu.SemaphoreType.DMA((2, ny)),
    ]
    vmem = pl.BlockSpec(memory_space=pltpu.VMEM)
    return pl.pallas_call(
        functools.partial(kernel, nx, ny),
        out_shape=(
            jax.ShapeDtypeStruct(source.shape, f32),
            jax.ShapeDtypeStruct((ex * QC, ey * QC, ez * QC), f32),
        ),
        in_specs=[vmem] * 3,
        out_specs=(vmem, vmem),
        scratch_shapes=scratch,
        compiler_params=pltpu.CompilerParams(
            collective_id=0, has_side_effects=True, vmem_limit_bytes=60 * 1024 * 1024
        ),
    )(source, conductivity, absorption)


def solution(mesh):
    spec = P("gx", "gy", None)
    return jax.shard_map(
        functools.partial(on_device, mesh.shape["gx"], mesh.shape["gy"]),
        mesh=mesh,
        in_specs=(spec,) * 3,
        out_specs=(spec, spec),
        check_vma=False,
    )
```

profile of v0, /device:TPU:0, one launch (start us, length us, event | category | flops | bytes accessed | tf_op | source)
XLA Modules:
  0.0 92.6 jit_solution(12819054397526330282)
XLA Ops:
  0.6 88.8 %shard_map.50 = (f32[20,20,640]{2,1,0:T(8,128)}, f32[12,12,384]{2,1,0:T(8,128)}) custom-call(f32[20,20,640]{2,1,0:T(8,128)} %src_ref.1, f32[20,20,640]{2,1,0:T(8,128)} %cond_ref.1, f32[20,20,640]{2,1,0:T(8,128)} %abs_ref.1), custom_call_target="tpu_custom_call" | custom-call | tf_op jit(solution)/shard_map/pallas_call | solution.py:675
  89.4 0.0 copy-start
  89.4 2.4 %copy.7 = f32[20,20,640]{2,1,0:T(8,128)} copy(f32[20,20,640]{2,1,0:T(8,128)} %get-tuple-element.4) | data formatting | bytes 2048000
  91.9 0.0 copy-done
  91.9 0.7 copy.8
Async XLA Ops:
  89.4 2.5 %copy-start = (f32[12,12,384]{2,1,0:T(8,128)S(1)}, f32[12,12,384]{2,1,0:T(8,128)}, u32[]{:S(2)}) copy-start(f32[12,12,384]{2,1,0:T(8,128)} %get-tuple-element.5) | copy-start | bytes 663556
where the time goes:
time: 92.7 us; the launch traced here: 92.6 us
  Pallas kernels  88.8 us (96%)
  local copies, waits for them, and re-layouts  3.16 us (3%)
    pallas_call x1, Pallas kernels, on_device(): pl.pallas_call(functools.partial(kernel, nx, ny), out_shape=(jax.ShapeDty...  88.8 us
    unnamed x4, local copies, waits for them, and re-layouts  3.16 us

commit v1 on v0

--- a/solution.py
+++ b/solution.py
@@ -10,7 +10,7 @@
 from jax.sharding import PartitionSpec as P
 
 SWEEPS = 3
-STAGES = 7
+STAGES = 10
 MESH = pl.DeviceIdType.MESH
 DIRS = [(-1, 0), (1, 0), (0, -1), (0, 1), (-1, -1), (-1, 1), (1, -1), (1, 1)]
 
@@ -127,15 +127,23 @@
 
         @pl.loop(0, q)
         def _(a, axis=axis):
-            for b in range(q):
+            def read(b):
                 start, step = plane_starts(q, axis, a, b)
                 u = [src[start + step * i] for i in range(q)]
+                base = None if axis == 0 else [dst[start + step * i] for i in range(q)]
+                return u, base
+
+            ahead = read(0)
+            for b in range(q):
+                u, base = ahead
+                if b + 1 < q:
+                    ahead = read(b + 1)
+                start, step = plane_starts(q, axis, a, b)
                 g = antisym(table, u)
                 g = [flux[start + step * i] * g[i] for i in range(q)]
                 r = antisym(table.T, g)
                 for i in range(q):
-                    base = mass[start + step * i] * u[i] if axis == 0 else dst[start + step * i]
-                    r[i] = base + r[i]
+                    r[i] = (mass[start + step * i] * u[i] if base is None else base[i]) + r[i]
                 if axis == 2:
                     r = z_sum(r, lanes)
                 for i in range(q):
@@ -175,7 +183,14 @@
     perm,
     back,
     cback,
-    fine,
+    load,
+    inv,
+    power,
+    w0,
+    w1,
+    w2,
+    b,
+    power_2,
     flux,
     mass,
     coarse,
@@ -430,7 +445,7 @@
                         raw[z, pl.ds(n * rows + at, ey, stride=QF), :] for n in range(3)
                     ]
                     place = slice(e * ey, (e + 1) * ey)
-                    fine[0, p, place, :] = weight * values[0]
+                    load[p, place, :] = weight * values[0]
                     flux[p, place, :] = weight * values[1]
                     mass[p, place, :] = weight * values[2]
                     if on_coarse:
@@ -440,8 +455,6 @@
                         cflux[cp, place, :] = cw * values[1]
                         cmass[cp, place, :] = cw * values[2]
 
-    load, inv, power, w0, w1, w2, b = [fine.at[i] for i in range(7)]
-    power_2 = fine.at[7]
     cinv, cur, crhs, cw0, cb, cpow, cw1, ccor = [coarse.at[i] for i in range(8)]
 
     def each(q, body):
@@ -467,7 +480,7 @@
         return body
 
     def restrict(field, dst):
-        for x in range(1):
+        if True:
 
             @pl.loop(0, QF)
             def _(a):
@@ -503,13 +516,18 @@
         load[a * QF] = line[0]
         load[a * QF + QF - 1] = line[-1]
 
+    pl.semaphore_wait(barrier, len(greeted))
+    load_fields = [(load, QF)]
+    load_copies = start_exchange(7, load_fields)
     local_diag(inv, flux, mass, FINE_D, lanes)
     local_diag(cinv, cflux, cmass, COARSE_D, lanes)
-    pl.semaphore_wait(barrier, len(greeted))
-    fields = [(load, QF), (inv, QF), (cinv, QC)]
+    fields = [(inv, QF), (cinv, QC)]
     copies = start_exchange(0, fields)
-    transposed_permutation(back, QF)
-    transposed_permutation(cback, QC)
+    finish_exchange(7, load_fields, load_copies)
+
+    apply_fine(load, power)
+    power_fields = [(power, QF)]
+    power_copies = start_exchange(8, power_fields)
     finish_exchange(0, fields, copies)
 
     def invert(p):
@@ -519,24 +537,30 @@
 
     each(QF, invert)
     each(QC, store(cinv, lambda p: 1.0 / cinv[p]))
-
-    apply_fine(load, power)
+    restrict(load, crhs)
     apply_fine(b, w0)
-    restrict(load, crhs)
-    fields = [(power, QF), (w0, QF), (crhs, QC)]
-    finish_exchange(1, fields, start_exchange(1, fields))
+    fields = [(w0, QF), (crhs, QC)]
+    copies = start_exchange(1, fields)
+
+    finish_exchange(8, power_fields, power_copies)
     each(QF, store(power, lambda p: inv[p] * power[p]))
+    apply_fine(power, power_2)
+    power_fields = [(power_2, QF)]
+    power_copies = start_exchange(9, power_fields)
+    sum_first = squares(QF, lambda p: power[p])
+
+    finish_exchange(1, fields, copies)
     each(QF, store(b, lambda p: inv[p] * w0[p]))
-
-    apply_fine(power, power_2)
+    apply_coarse(crhs, cpow)
     apply_fine(b, w1)
-    apply_coarse(crhs, cpow)
-    fields = [(power_2, QF), (w1, QF), (cpow, QC)]
+    fields = [(w1, QF), (cpow, QC)]
     copies = start_exchange(2, fields)
-    sum_first = squares(QF, lambda p: power[p])
-    finish_exchange(2, fields, copies)
+    finish_exchange(9, power_fields, power_copies)
     sum_second = squares(QF, lambda p: inv[p] * power_2[p])
     line = start_line(0, True, sum_first, sum_second)
+    transposed_permutation(back, QF)
+    transposed_permutation(cback, QC)
+    finish_exchange(2, fields, copies)
     each(QF, store(b, lambda p: inv[p] * w1[p]))
     each(QC, store(cpow, lambda p: cinv[p] * cpow[p]))
 
@@ -640,7 +664,7 @@
     subs = ex * ey
     rows = px * (-(-py // 8) * 8)
     crows = ex * QC * (-(-ey * QC // 8) * 8)
-    tiles = -(-(2 * QF * QF + QC * QC) // min(ex, ey))
+    tiles = -(-(QF * QF + QC * QC) // min(ex, ey))
     f32, bf16 = jnp.float32, jnp.bfloat16
     dirs = len(DIRS)
     longest = max(nx, ny)
@@ -651,7 +675,7 @@
         pltpu.VMEM((pz, pz), bf16),
         pltpu.VMEM((pz, pz), bf16),
         pltpu.VMEM((QC * ez, QC * ez), bf16),
-        pltpu.VMEM((8, QF**3, subs, ez), f32),
+        *[pltpu.VMEM((QF**3, subs, ez), f32)] * 8,
         pltpu.VMEM((QF**3, subs, ez), f32),
         pltpu.VMEM((QF**3, subs, ez), f32),
         pltpu.VMEM((8, QC**3, subs, ez), f32),

time: 92.7 us -> 82.8 us (0.89)
  Pallas kernels: 88.8 us -> 78.8 us
    pallas_call x1, Pallas kernels: 88.8 us -> 78.8 us  [on_device(): pl.pallas_call(functools.partial(kernel, nx, ny), out_shape=(jax.ShapeDty...]
where the time goes in v1:
time: 82.8 us; the launch traced here: 82.6 us
  Pallas kernels  78.8 us (95%)
  local copies, waits for them, and re-layouts  3.16 us (4%)
    pallas_call x1, Pallas kernels, on_device(): pl.pallas_call(functools.partial(kernel, nx, ny), out_shape=(jax.ShapeDty...  78.8 us
    unnamed x4, local copies, waits for them, and re-layouts  3.16 us

profile of v1, /device:TPU:0, one launch (start us, length us, event | category | flops | bytes accessed | tf_op | source)
XLA Modules:
  0.0 82.6 jit_solution(16899178969283959669)
XLA Ops:
  0.6 78.8 %shard_map.50 = (f32[20,20,640]{2,1,0:T(8,128)}, f32[12,12,384]{2,1,0:T(8,128)}) custom-call(f32[20,20,640]{2,1,0:T(8,128)} %src_ref.1, f32[20,20,640]{2,1,0:T(8,128)} %cond_ref.1, f32[20,20,640]{2,1,0:T(8,128)} %abs_ref.1), custom_call_target="tpu_custom_call" | custom-call | tf_op jit(solution)/shard_map/pallas_call | solution.py:699
  79.4 0.0 copy-start
  79.5 2.4 %copy.7 = f32[20,20,640]{2,1,0:T(8,128)} copy(f32[20,20,640]{2,1,0:T(8,128)} %get-tuple-element.4) | data formatting | bytes 2048000
  81.9 0.0 copy-done
  81.9 0.7 copy.8
Async XLA Ops:
  79.4 2.5 %copy-start = (f32[12,12,384]{2,1,0:T(8,128)S(1)}, f32[12,12,384]{2,1,0:T(8,128)}, u32[]{:S(2)}) copy-start(f32[12,12,384]{2,1,0:T(8,128)} %get-tuple-element.5) | copy-start | bytes 663556
